TPU v7x, 32 devices: a whole 2x2x4 slice. The times are simulated.
32 devices in a mesh: dp: 8 (over z, y), rep: 4 (over x, core).
Axes of the slice: x: 2, y: 2, z: 4, core: 2. Of those that a mesh axis runs over, the one named last changes fastest.
Arguments:
- circuits: bfloat16 [8192, 1024], P(('dp', 'rep')), may hold values from -2.65 to 2.65
- records: bfloat16 [8192, 1024], P(('dp', 'rep')), may hold values from -0.25 to 0.25
- record_gain: float32 [1024], replicated, may hold values from 0.5 to 2
- log_scale: float32 [1], replicated, may hold values from 1.6 to 2.4
- logit_bias: float32 [1], replicated, may hold values from -3 to -1
- hard_ids: int32 [8192, 16], P(('dp', 'rep')), may hold values from -1 to 8191, as said below
Outputs:
- grad_circuits: float32 [8192, 1024], P(('dp', 'rep'))
- grad_records: float32 [8192, 1024], P(('dp', 'rep'))
- grad_gain: float32 [1024], replicated
- statistics: float32 [2], replicated
- mean_loss: float32 [1], replicated
Inputs may be any that keep to these rules, and one draw needn't show every extreme that they name: `hard_ids`: every entry that is not -1 names a row held by a device with the same dp index as the pair's device (the same value of row // 1024). Over the 256 pairs of one device, at most 16 entries name rows of any one device, and in each dp index one device is named exactly 16 times by every device of that dp index.
All inputs are finite; a program needn't handle non-finite values.
Results may differ from a plain program's by a relative error of at most 0.0043.
Values may be sent and summed in bfloat16 or wider, within the bound.
A program may use at most 64 MiB of HBM per device.

v0:
```python
import jax
import jax.numpy as jnp
from jax import lax
from jax.sharding import PartitionSpec as P

HOPS = 4
CAP = 16
EPSILON = 1e-06


def shifted(value, axis, steps):
    count = lax.axis_size(axis)
    pairs = [(source, (source + steps) % count) for source in range(count)]
    return lax.ppermute(value, axis, pairs)


def unit_rows(values):
    sq_total = jnp.sum(values * values, axis=-1, keepdims=True)
    lengths = jnp.sqrt(sq_total + EPSILON)
    return (values / lengths, lengths)


def transposed_product(left, right):
    return lax.dot_general(
        left, right, (((0,), (0,)), ((), ())), preferred_element_type=jnp.float32
    )


def score_tile(circ_block, rec_block, multiplier, bias_value, own_block):
    products = lax.dot_general(
        circ_block, rec_block, (((1,), (1,)), ((), ())), preferred_element_type=jnp.float32
    )
    scores = products * multiplier + bias_value
    weights = jax.nn.sigmoid(scores)
    losses = jax.nn.softplus(scores)
    if own_block:
        tile_rows = scores.shape[0]
        diag_mask = (
            lax.broadcasted_iota(jnp.int32, (tile_rows, tile_rows), 0)
            == lax.broadcasted_iota(jnp.int32, (tile_rows, tile_rows), 1)
        ).astype(jnp.float32)
        weights = weights - diag_mask
        losses = losses - scores * diag_mask
    summary = jnp.stack(
        [jnp.sum(weights * (scores - bias_value)), jnp.sum(weights), jnp.sum(losses)]
    )
    return (weights.astype(jnp.bfloat16), summary)


def per_device(circuits, records, record_gain, log_scale, logit_bias, hard_ids):
    pair_rows = circuits.shape[0]
    list_width = hard_ids.shape[1]
    rep_count = lax.axis_size("rep")
    loop_count = lax.axis_size("dp")
    circ_unit, circ_length = unit_rows(circuits.astype(jnp.float32))
    circ_emb = circ_unit.astype(jnp.bfloat16)
    rec_pre = records.astype(jnp.float32) * record_gain
    rec_unit, rec_length = unit_rows(rec_pre)
    rec_emb = rec_unit.astype(jnp.bfloat16)
    multiplier = jnp.exp(log_scale[0])
    bias_value = logit_bias[0]
    own_weights, summary = score_tile(circ_emb, rec_emb, multiplier, bias_value, True)
    grad_circ = jnp.dot(own_weights, rec_emb, preferred_element_type=jnp.float32)
    running = transposed_product(own_weights, circ_emb)
    visitor = rec_emb
    for hop_index in range(HOPS):
        visitor = shifted(visitor, "dp", -1)
        running = shifted(running, "dp", -1)
        weights, portion = score_tile(circ_emb, visitor, multiplier, bias_value, False)
        grad_circ = grad_circ + jnp.dot(weights, visitor, preferred_element_type=jnp.float32)
        summary = summary + portion
        running = running + transposed_product(weights, circ_emb)
    grad_rec = shifted(running, "dp", HOPS)
    entry_ids = hard_ids.reshape(-1)
    entry_count = entry_ids.shape[0]
    is_live = entry_ids >= 0
    owner_dev = entry_ids // pair_rows % rep_count
    row_within = entry_ids % pair_rows
    owner_hits = (
        (owner_dev[:, None] == jnp.arange(rep_count, dtype=jnp.int32)[None, :]) & is_live[:, None]
    ).astype(jnp.int32)
    before = jnp.cumsum(owner_hits, axis=0) - owner_hits
    slot_index = jnp.sum(before * owner_hits, axis=1)
    slot_total = rep_count * CAP
    target = jnp.where(is_live, owner_dev * CAP + slot_index, slot_total)
    asked_rows = (
        jnp.zeros((slot_total,), jnp.int32)
        .at[target]
        .set(row_within, mode="drop")
        .reshape(rep_count, CAP)
    )
    slot_pair = (
        jnp.zeros((slot_total,), jnp.int32)
        .at[target]
        .set(jnp.arange(entry_count, dtype=jnp.int32) // list_width, mode="drop")
    )
    slot_live = jnp.zeros((slot_total,), jnp.float32).at[target].set(1.0, mode="drop")
    found_rows = jnp.take(
        rec_emb, lax.all_to_all(asked_rows, "rep", split_axis=0, concat_axis=0, tiled=True), axis=0
    )
    fetched = lax.all_to_all(found_rows, "rep", split_axis=0, concat_axis=0, tiled=True)
    fetched = fetched.reshape(slot_total, fetched.shape[2])
    slot_products = lax.dot_general(
        fetched, circ_emb, (((1,), (1,)), ((), ())), preferred_element_type=jnp.float32
    )
    chosen = (slot_pair[:, None] == lax.broadcasted_iota(jnp.int32, (slot_total, pair_rows), 1)) & (
        slot_live[:, None] > 0
    )
    hard_products = jnp.sum(jnp.where(chosen, slot_products, 0.0), axis=1)
    hard_scores = hard_products * multiplier + bias_value
    hard_weights = jnp.where(slot_live > 0, jax.nn.sigmoid(hard_scores), 0.0)
    hard_losses = jnp.where(slot_live > 0, jax.nn.softplus(hard_scores), 0.0)
    spread = jnp.where(
        chosen, hard_weights.astype(jnp.bfloat16)[:, None], jnp.zeros((), jnp.bfloat16)
    )
    hard_grad = transposed_product(spread, fetched)
    summary = summary + jnp.stack(
        [
            jnp.sum(hard_weights * hard_products * multiplier),
            jnp.sum(hard_weights),
            jnp.sum(hard_losses),
        ]
    )
    grad_circ_emb = multiplier * (grad_circ + hard_grad)
    grad_rec_emb = multiplier * grad_rec
    grad_circuits = (
        grad_circ_emb - circ_unit * jnp.sum(circ_unit * grad_circ_emb, axis=-1, keepdims=True)
    ) / circ_length
    grad_pre = (
        grad_rec_emb - rec_unit * jnp.sum(rec_unit * grad_rec_emb, axis=-1, keepdims=True)
    ) / rec_length
    grad_records = grad_pre * record_gain
    gain_part = jnp.sum(records.astype(jnp.float32) * grad_pre, axis=0)
    gain_total, summary_total = lax.psum((gain_part, summary), ("dp", "rep"))
    pair_total = pair_rows * loop_count * rep_count
    statistics = jnp.stack([summary_total[0], summary_total[1]])
    mean_loss = jnp.stack([summary_total[2] / pair_total])
    return (grad_circuits, grad_records, gain_total, statistics, mean_loss)


def solution(mesh):
    placed = (P(("dp", "rep"), None), P(("dp", "rep"), None), P(), P(), P(), P(("dp", "rep"), None))
    return jax.shard_map(
        per_device,
        mesh=mesh,
        in_specs=placed,
        out_specs=(P(("dp", "rep"), None), P(("dp", "rep"), None), P(), P(), P()),
        check_vma=False,
    )
```

profile of v0, /device:TPU:12, one launch (start us, length us, event | category | flops | bytes accessed | tf_op | source)
XLA Modules:
  0.0 262.5 jit_solution(4319335786389604963)
XLA Ops:
  3.9 15.5 %scatter_custom_fusion.2 = s32[64]{0:T(128)S(1)} fusion(s32[4096]{0:T(1024)S(1)} %bitcast.84, s32[4096]{0:T(1024)S(1)} %get-tuple-element.28, s32[]{:T(128)} %constant.87.clone.1), kind=kCustom, calls=%fused_computation.158 | custom fusion | bytes 260 | tf_op jit(solution)/shard_map/scatter | solution.py:89
  20.0 3.2 %all-to-all-start = ((s32[4,1,16]{2,1,0:T(1,128)}), s32[4,1,16]{2,1,0:T(1,128)S(1)}, u32[]{:S(2)}, u32[]{:S(2)}) async-start(s32[4,1,16]{2,1,0:T(1,128)} %bitcast.5), calls=%async_computation | async-start | bytes 4096 | tf_op jit(solution)/shard_map/all_to_all | solution.py:99
  30.0 15.5 %scatter_custom_fusion.1 = f32[64]{0:T(128)S(1)} fusion(s32[4096]{0:T(1024)S(1)} %bitcast.85, f32[4096]{0:T(1024)S(1)} %broadcast.271, f32[]{:T(128)} %constant.85.clone.1), kind=kCustom, calls=%fused_computation.156 | custom fusion | bytes 260 | tf_op jit(solution)/shard_map/scatter | solution.py:97
  46.5 16.0 %scatter_custom_fusion = s32[64]{0:T(128)} fusion(s32[4096]{0:T(1024)S(1)} %bitcast.86, s32[4096]{0:T(1024)S(1)} %add_select_fusion.1, s32[]{:T(128)} %constant.87.clone.1), kind=kCustom, calls=%fused_computation.160 | custom fusion | bytes 260 | tf_op jit(solution)/shard_map/scatter | solution.py:95
  63.4 2.3 multiply_reduce_fusion.5
  65.7 2.5 convolution_add_fusion
  68.3 4.3 %collective-permute-start.5 = (f32[256,1024]{1,0:T(8,128)}, f32[256,1024]{1,0:T(8,128)}, u32[]{:S(2)}, u32[]{:S(2)}) collective-permute-start(f32[256,1024]{1,0:T(8,128)} %convolution_add_fusion), channel_id=1, source_target_pairs={{0,28},{4,0},{8,4},{12,8},{16,12},{20,16},{24,20},{28,24},{1,29},{... | collective-permute-start | bytes 3145736 | tf_op jit(solution)/shard_map/ppermute | solution.py:14
  74.7 3.3 %all-to-all-start.1 = ((bf16[4,16,1024]{2,1,0:T(8,128)(2,1)}), bf16[4,16,1024]{2,1,0:T(8,128)(2,1)S(1)}, u32[]{:S(2)}, u32[]{:S(2)}) async-start(bf16[4,16,1024]{2,1,0:T(8,128)(2,1)} %broadcast_select_fusion), calls=%async_computation.1 | async-start | bytes 262144 | tf_op jit(solution)/shard_map/all_to_all | solution.py:101
  78.6 2.3 multiply_reduce_fusion.4
  81.2 1.7 collective-permute-start.2
  83.0 18.1 %collective-permute-done.5 = f32[256,1024]{1,0:T(8,128)} collective-permute-done((f32[256,1024]{1,0:T(8,128)}, f32[256,1024]{1,0:T(8,128)}, u32[]{:S(2)}, u32[]{:S(2)}) %collective-permute-start.5) | collective-permute-done | bytes 1048608 | tf_op jit(solution)/shard_map/ppermute | solution.py:14
  101.1 2.3 add.241
  103.4 1.7 collective-permute-start.6
  107.2 5.2 %collective-permute-done.2 = bf16[256,1024]{1,0:T(8,128)(2,1)} collective-permute-done((bf16[256,1024]{1,0:T(8,128)(2,1)}, bf16[256,1024]{1,0:T(8,128)(2,1)}, u32[]{:S(2)}, u32[]{:S(2)}) %collective-permute-start.2) | collective-permute-done | bytes 524320 | tf_op jit(solution)/shard_map/ppermute | solution.py:14
  112.3 1.7 collective-permute-start.3
  114.0 2.2 multiply_reduce_fusion.3
  116.6 18.2 %collective-permute-done.6 = f32[256,1024]{1,0:T(8,128)} collective-permute-done((f32[256,1024]{1,0:T(8,128)}, f32[256,1024]{1,0:T(8,128)}, u32[]{:S(2)}, u32[]{:S(2)}) %collective-permute-start.6) | collective-permute-done | bytes 1048608 | tf_op jit(solution)/shard_map/ppermute | solution.py:14
  136.2 1.9 collective-permute-start.7
  140.8 5.1 %collective-permute-done.3 = bf16[256,1024]{1,0:T(8,128)(2,1)S(1)} collective-permute-done((bf16[256,1024]{1,0:T(8,128)(2,1)}, bf16[256,1024]{1,0:T(8,128)(2,1)S(1)}, u32[]{:S(2)}, u32[]{:S(2)}) %collective-permute-start.3) | collective-permute-done | bytes 524320 | tf_op jit(solution)/shard_map/ppermute | solution.py:14
  147.5 19.8 %collective-permute-done.7 = f32[256,1024]{1,0:T(8,128)S(1)} collective-permute-done((f32[256,1024]{1,0:T(8,128)S(1)}, f32[256,1024]{1,0:T(8,128)S(1)}, u32[]{:S(2)}, u32[]{:S(2)}) %collective-permute-start.7) | collective-permute-done | bytes 1048608 | tf_op jit(solution)/shard_map/ppermute | solution.py:14
  167.5 4.5 %collective-permute-start.8 = (f32[256,1024]{1,0:T(8,128)S(1)}, f32[256,1024]{1,0:T(8,128)S(1)}, u32[]{:S(2)}, u32[]{:S(2)}) collective-permute-start(f32[256,1024]{1,0:T(8,128)S(1)} %add.243), channel_id=1, source_target_pairs={{0,16},{4,20},{8,24},{12,28},{16,0},{20,4},{24,8},{28,12},{1,17},{... | collective-permute-start | bytes 3145736 | tf_op jit(solution)/shard_map/ppermute | solution.py:14
  173.3 11.6 %fusion.63 = f32[3]{0:T(128)S(1)} fusion(f32[1]{0:T(128)} %bitcast.24, f32[1]{0:T(128)} %bitcast.23, f32[1]{0:T(128)} %bitcast.22, f32[1]{0:T(128)} %bitcast.27, f32[1]{0:T(128)} %bitcast.26, f32[1]{0:T(128)} %bitcast.25, f32[1]{0:T(128)} %bitcast.21, f32[1]{0:T(128)} %bitcast.20, f32[1]{0:T(128)} %bitcast.19, f32[1]{0:T(128)} %bitcast.18, f32[1]{0:T(128)} %bitcast.17, ...), kind=kLoop, calls=%fused_computation.151 | loop fusion | flops 51 | bytes 84 | tf_op jit(solution)/shard_map/add | solution.py:117
  186.6 28.4 %collective-permute-done.8 = f32[256,1024]{1,0:T(8,128)S(1)} collective-permute-done((f32[256,1024]{1,0:T(8,128)S(1)}, f32[256,1024]{1,0:T(8,128)S(1)}, u32[]{:S(2)}, u32[]{:S(2)}) %collective-permute-start.8) | collective-permute-done | bytes 1048608 | tf_op jit(solution)/shard_map/ppermute | solution.py:14
  216.8 42.8 %all-reduce = (f32[1024]{0:T(1024)}, f32[3]{0:T(128)S(1)}) all-reduce(f32[1024]{0:T(1024)S(1)} %get-tuple-element.26, f32[3]{0:T(128)S(1)} %fusion.63), channel_id=1, replica_groups=mesh['dp'=8,'rep'=4] {'dp','rep'}, use_global_device_ids=true, to_apply=%region_12.13 | all-reduce | flops 1027 | bytes 8216 | tf_op jit(solution)/shard_map/psum | solution.py:134
  (76 shorter events, 28.3 us)
Async XLA Ops:
  1.6 21.7 %copy-start = (bf16[256,1024]{1,0:T(8,128)(2,1)S(1)}, bf16[256,1024]{1,0:T(8,128)(2,1)}, u32[]{:S(2)}) copy-start(bf16[256,1024]{1,0:T(8,128)(2,1)} %param.7) | copy-start | bytes 1572868
  19.4 3.9 %copy-start.2 = (f32[1024]{0:T(1024)S(1)}, f32[1024]{0:T(1024)}, u32[]{:S(2)}) copy-start(f32[1024]{0:T(1024)} %param.8) | copy-start | bytes 12292
  20.0 42.5 %all-to-all-start = ((s32[4,1,16]{2,1,0:T(1,128)}), s32[4,1,16]{2,1,0:T(1,128)S(1)}, u32[]{:S(2)}, u32[]{:S(2)}) async-start(s32[4,1,16]{2,1,0:T(1,128)} %bitcast.5), calls=%async_computation | async-start | bytes 4096 | tf_op jit(solution)/shard_map/all_to_all | solution.py:99
  23.5 1.0 copy-start.1
  23.7 38.9 %collective-permute-start = (bf16[256,1024]{1,0:T(8,128)(2,1)S(1)}, bf16[256,1024]{1,0:T(8,128)(2,1)}, u32[]{:S(2)}, u32[]{:S(2)}) collective-permute-start(bf16[256,1024]{1,0:T(8,128)(2,1)S(1)} %fusion.77), channel_id=1, source_target_pairs={{0,28},{4,0},{8,4},{12,8},{16,12},{20,16},{24,20},{28,24},{1,29},{... | collective-permute-start | bytes 1572872 | tf_op jit(solution)/shard_map/ppermute | solution.py:14
  28.9 36.8 %collective-permute-start.4 = (f32[256,1024]{1,0:T(8,128)}, f32[256,1024]{1,0:T(8,128)}, u32[]{:S(2)}, u32[]{:S(2)}) collective-permute-start(f32[256,1024]{1,0:T(8,128)} %fusion.33), channel_id=1, source_target_pairs={{0,28},{4,0},{8,4},{12,8},{16,12},{20,16},{24,20},{28,24},{1,29},{... | collective-permute-start | bytes 3145736 | tf_op jit(solution)/shard_map/ppermute | solution.py:14
  45.5 0.5 copy-start.5
  62.6 16.0 %collective-permute-start.1 = (bf16[256,1024]{1,0:T(8,128)(2,1)}, bf16[256,1024]{1,0:T(8,128)(2,1)}, u32[]{:S(2)}, u32[]{:S(2)}) collective-permute-start(bf16[256,1024]{1,0:T(8,128)(2,1)} %collective-permute-done), channel_id=1, source_target_pairs={{0,28},{4,0},{8,4},{12,8},{16,12},{20,16},{24,20},{28,24},{1,29},{... | collective-permute-start | bytes 1572872 | tf_op jit(solution)/shard_map/ppermute | solution.py:14
  68.3 32.9 %collective-permute-start.5 = (f32[256,1024]{1,0:T(8,128)}, f32[256,1024]{1,0:T(8,128)}, u32[]{:S(2)}, u32[]{:S(2)}) collective-permute-start(f32[256,1024]{1,0:T(8,128)} %convolution_add_fusion), channel_id=1, source_target_pairs={{0,28},{4,0},{8,4},{12,8},{16,12},{20,16},{24,20},{28,24},{1,29},{... | collective-permute-start | bytes 3145736 | tf_op jit(solution)/shard_map/ppermute | solution.py:14
  74.7 30.4 %all-to-all-start.1 = ((bf16[4,16,1024]{2,1,0:T(8,128)(2,1)}), bf16[4,16,1024]{2,1,0:T(8,128)(2,1)S(1)}, u32[]{:S(2)}, u32[]{:S(2)}) async-start(bf16[4,16,1024]{2,1,0:T(8,128)(2,1)} %broadcast_select_fusion), calls=%async_computation.1 | async-start | bytes 262144 | tf_op jit(solution)/shard_map/all_to_all | solution.py:101
  81.2 31.1 %collective-permute-start.2 = (bf16[256,1024]{1,0:T(8,128)(2,1)}, bf16[256,1024]{1,0:T(8,128)(2,1)}, u32[]{:S(2)}, u32[]{:S(2)}) collective-permute-start(bf16[256,1024]{1,0:T(8,128)(2,1)} %collective-permute-done.1), channel_id=1, source_target_pairs={{0,28},{4,0},{8,4},{12,8},{16,12},{20,16},{24,20},{28,24},{1,29},{... | collective-permute-start | bytes 1572872 | tf_op jit(solution)/shard_map/ppermute | solution.py:14
  103.4 1.7 copy-start.3
  103.4 1.7 copy-start.4
  103.4 31.4 %collective-permute-start.6 = (f32[256,1024]{1,0:T(8,128)}, f32[256,1024]{1,0:T(8,128)}, u32[]{:S(2)}, u32[]{:S(2)}) collective-permute-start(f32[256,1024]{1,0:T(8,128)} %add.241), channel_id=1, source_target_pairs={{0,28},{4,0},{8,4},{12,8},{16,12},{20,16},{24,20},{28,24},{1,29},{... | collective-permute-start | bytes 3145736 | tf_op jit(solution)/shard_map/ppermute | solution.py:14
  105.5 0.6 copy-start.6
  112.3 33.6 %collective-permute-start.3 = (bf16[256,1024]{1,0:T(8,128)(2,1)}, bf16[256,1024]{1,0:T(8,128)(2,1)S(1)}, u32[]{:S(2)}, u32[]{:S(2)}) collective-permute-start(bf16[256,1024]{1,0:T(8,128)(2,1)} %collective-permute-done.2), channel_id=1, source_target_pairs={{0,28},{4,0},{8,4},{12,8},{16,12},{20,16},{24,20},{28,24},{1,29},{... | collective-permute-start | bytes 1572872 | tf_op jit(solution)/shard_map/ppermute | solution.py:14
  136.2 31.1 %collective-permute-start.7 = (f32[256,1024]{1,0:T(8,128)S(1)}, f32[256,1024]{1,0:T(8,128)S(1)}, u32[]{:S(2)}, u32[]{:S(2)}) collective-permute-start(f32[256,1024]{1,0:T(8,128)S(1)} %add.242), channel_id=1, source_target_pairs={{0,28},{4,0},{8,4},{12,8},{16,12},{20,16},{24,20},{28,24},{1,29},{... | collective-permute-start | bytes 3145736 | tf_op jit(solution)/shard_map/ppermute | solution.py:14
  167.5 47.5 %collective-permute-start.8 = (f32[256,1024]{1,0:T(8,128)S(1)}, f32[256,1024]{1,0:T(8,128)S(1)}, u32[]{:S(2)}, u32[]{:S(2)}) collective-permute-start(f32[256,1024]{1,0:T(8,128)S(1)} %add.243), channel_id=1, source_target_pairs={{0,16},{4,20},{8,24},{12,28},{16,0},{20,4},{24,8},{28,12},{1,17},{... | collective-permute-start | bytes 3145736 | tf_op jit(solution)/shard_map/ppermute | solution.py:14
  259.6 0.5 copy-start.7
where the time goes:
time: 264 us; the launch traced here: 263 us
  waiting for transfers between devices  95.5 us (36%)
  local copies, waits for them, and re-layouts  52.1 us (20%)
  blocking collectives  42.8 us (16%)
  starting transfers between devices  24.7 us (9%)
  other arithmetic  23.6 us (9%)
  matrix products  19.7 us (7%)
  between operations  4.03 us (2%)
    ppermute x9, waiting for transfers between devices, shifted(): return lax.ppermute(value, axis, pairs)  95.5 us
    psum x1, blocking collectives, per_device(): gain_total, summary_total = lax.psum((gain_part, summary), ('dp', 'rep'))  42.8 us
    ppermute x9, starting transfers between devices, shifted(): return lax.ppermute(value, axis, pairs)  18.2 us
    scatter x1, local copies, waits for them, and re-layouts, per_device(): slot_pair = jnp.zeros((slot_total,), jnp.int32).at[target].set(jnp.arange...  16 us
    scatter x1, local copies, waits for them, and re-layouts, per_device(): asked_rows = jnp.zeros((slot_total,), jnp.int32).at[target].set(row_withi...  15.5 us
    scatter x1, local copies, waits for them, and re-layouts, per_device(): jnp.zeros((slot_total,), jnp.float32).at[target].set(1.0, mode='drop')  15.5 us
    add x1, other arithmetic, per_device(): summary + jnp.stack([jnp.sum(hard_weights * hard_products * multiplier),...  11.6 us
    dot_general x5, matrix products, score_tile(): lax.dot_general(circ_block, rec_block, (((1,), (1,)), ((), ())), preferre...  9.18 us
  transfers between devices with their start and end apart: 11, of which 7 were waited for; matrix products, arithmetic and copies ran while one was open for 27% of the time, Pallas kernels for 0%

commit v1 on v0

--- a/solution.py
+++ b/solution.py
@@ -131,7 +131,7 @@
     ) / rec_length
     grad_records = grad_pre * record_gain
     gain_part = jnp.sum(records.astype(jnp.float32) * grad_pre, axis=0)
-    gain_total, summary_total = lax.psum((gain_part, summary), ("dp", "rep"))
+    gain_total, summary_total = lax.psum(lax.psum((gain_part, summary), "rep"), "dp")
     pair_total = pair_rows * loop_count * rep_count
     statistics = jnp.stack([summary_total[0], summary_total[1]])
     mean_loss = jnp.stack([summary_total[2] / pair_total])

time: 264 us -> 252 us (0.955)
  the two profiles are of different devices: /device:TPU:12 before, /device:TPU:0 now
where the time goes in v1:
time: 252 us; the launch traced here: 251 us
  waiting for transfers between devices  93.2 us (37%)
  local copies, waits for them, and re-layouts  51.8 us (21%)
  starting transfers between devices  31.1 us (12%)
  blocking collectives  27.8 us (11%)
  other arithmetic  23.6 us (9%)
  matrix products  19.7 us (8%)
  between operations  4.02 us (2%)
    ppermute x9, waiting for transfers between devices, shifted(): return lax.ppermute(value, axis, pairs)  93.1 us
    ppermute x9, starting transfers between devices, shifted(): return lax.ppermute(value, axis, pairs)  23.5 us
    psum x1, blocking collectives, per_device(): lax.psum(lax.psum((gain_part, summary), 'rep'), 'dp')  21 us
    scatter x1, local copies, waits for them, and re-layouts, per_device(): slot_pair = jnp.zeros((slot_total,), jnp.int32).at[target].set(jnp.arange...  16 us
    scatter x1, local copies, waits for them, and re-layouts, per_device(): asked_rows = jnp.zeros((slot_total,), jnp.int32).at[target].set(row_withi...  15.5 us
    scatter x1, local copies, waits for them, and re-layouts, per_device(): jnp.zeros((slot_total,), jnp.float32).at[target].set(1.0, mode='drop')  15.5 us
    add x1, other arithmetic, per_device(): summary + jnp.stack([jnp.sum(hard_weights * hard_products * multiplier),...  11.6 us
    dot_general x5, matrix products, score_tile(): lax.dot_general(circ_block, rec_block, (((1,), (1,)), ((), ())), preferre...  9.19 us
  transfers between devices with their start and end apart: 11, of which 7 were waited for; matrix products, arithmetic and copies ran while one was open for 29% of the time, Pallas kernels for 0%

profile of v1, /device:TPU:0, one launch (start us, length us, event | category | flops | bytes accessed | tf_op | source)
XLA Modules:
  0.0 251.2 jit_solution(9487909984934260542)
XLA Ops:
  3.9 15.5 %scatter_custom_fusion.2 = s32[64]{0:T(128)S(1)} fusion(s32[4096]{0:T(1024)S(1)} %bitcast.84, s32[4096]{0:T(1024)S(1)} %get-tuple-element.30, s32[]{:T(128)} %constant.87.clone.1), kind=kCustom, calls=%fused_computation.158 | custom fusion | bytes 260 | tf_op jit(solution)/shard_map/scatter | solution.py:89
  20.0 4.2 %all-to-all-start = ((s32[4,1,16]{2,1,0:T(1,128)}), s32[4,1,16]{2,1,0:T(1,128)S(1)}, u32[]{:S(2)}, u32[]{:S(2)}) async-start(s32[4,1,16]{2,1,0:T(1,128)} %bitcast.5), calls=%async_computation | async-start | bytes 4096 | tf_op jit(solution)/shard_map/all_to_all | solution.py:99
  24.7 5.1 %collective-permute-start = (bf16[256,1024]{1,0:T(8,128)(2,1)S(1)}, bf16[256,1024]{1,0:T(8,128)(2,1)}, u32[]{:S(2)}, u32[]{:S(2)}) collective-permute-start(bf16[256,1024]{1,0:T(8,128)(2,1)S(1)} %fusion.77), channel_id=1, source_target_pairs={{0,28},{4,0},{8,4},{12,8},{16,12},{20,16},{24,20},{28,24},{1,29},{... | collective-permute-start | bytes 1572872 | tf_op jit(solution)/shard_map/ppermute | solution.py:14
  34.9 15.5 %scatter_custom_fusion.1 = f32[64]{0:T(128)S(1)} fusion(s32[4096]{0:T(1024)S(1)} %bitcast.85, f32[4096]{0:T(1024)S(1)} %broadcast.271, f32[]{:T(128)} %constant.85.clone.1), kind=kCustom, calls=%fused_computation.156 | custom fusion | bytes 260 | tf_op jit(solution)/shard_map/scatter | solution.py:97
  51.4 16.0 %scatter_custom_fusion = s32[64]{0:T(128)} fusion(s32[4096]{0:T(1024)S(1)} %bitcast.86, s32[4096]{0:T(1024)S(1)} %add_select_fusion.1, s32[]{:T(128)} %constant.87.clone.1), kind=kCustom, calls=%fused_computation.160 | custom fusion | bytes 260 | tf_op jit(solution)/shard_map/scatter | solution.py:95
  68.6 2.3 multiply_reduce_fusion.5
  70.9 2.5 %convolution_add_fusion = f32[256,1024]{1,0:T(8,128)} fusion(f32[256,1024]{1,0:T(8,128)} %collective-permute-done.4, bf16[256,1024]{1,0:T(8,128)(2,1)S(1)} %fusion.72, f32[256,256]{1,0:T(8,128)S(1)} %get-tuple-element.37), kind=kOutput, calls=%fused_computation.4 | convolution fusion | flops 134742016 | bytes 2883584 | tf_op jit(solution)/shard_map/dot_general | solution.py:24
  76.4 3.3 %all-to-all-start.1 = ((bf16[4,16,1024]{2,1,0:T(8,128)(2,1)}), bf16[4,16,1024]{2,1,0:T(8,128)(2,1)S(1)}, u32[]{:S(2)}, u32[]{:S(2)}) async-start(bf16[4,16,1024]{2,1,0:T(8,128)(2,1)} %broadcast_select_fusion), calls=%async_computation.1 | async-start | bytes 262144 | tf_op jit(solution)/shard_map/all_to_all | solution.py:101
  79.8 2.8 %collective-permute-done.1 = bf16[256,1024]{1,0:T(8,128)(2,1)} collective-permute-done((bf16[256,1024]{1,0:T(8,128)(2,1)}, bf16[256,1024]{1,0:T(8,128)(2,1)}, u32[]{:S(2)}, u32[]{:S(2)}) %collective-permute-start.1) | collective-permute-done | bytes 524320 | tf_op jit(solution)/shard_map/ppermute | solution.py:14
  82.6 2.3 multiply_reduce_fusion.4
  85.2 3.9 %collective-permute-start.2 = (bf16[256,1024]{1,0:T(8,128)(2,1)}, bf16[256,1024]{1,0:T(8,128)(2,1)}, u32[]{:S(2)}, u32[]{:S(2)}) collective-permute-start(bf16[256,1024]{1,0:T(8,128)(2,1)} %collective-permute-done.1), channel_id=1, source_target_pairs={{0,28},{4,0},{8,4},{12,8},{16,12},{20,16},{24,20},{28,24},{1,29},{... | collective-permute-start | bytes 1572872 | tf_op jit(solution)/shard_map/ppermute | solution.py:14
  89.1 16.0 %collective-permute-done.5 = f32[256,1024]{1,0:T(8,128)} collective-permute-done((f32[256,1024]{1,0:T(8,128)}, f32[256,1024]{1,0:T(8,128)}, u32[]{:S(2)}, u32[]{:S(2)}) %collective-permute-start.5) | collective-permute-done | bytes 1048608 | tf_op jit(solution)/shard_map/ppermute | solution.py:14
  105.1 2.3 add.245
  107.4 3.8 %collective-permute-start.6 = (f32[256,1024]{1,0:T(8,128)}, f32[256,1024]{1,0:T(8,128)}, u32[]{:S(2)}, u32[]{:S(2)}) collective-permute-start(f32[256,1024]{1,0:T(8,128)} %add.245), channel_id=1, source_target_pairs={{0,28},{4,0},{8,4},{12,8},{16,12},{20,16},{24,20},{28,24},{1,29},{... | collective-permute-start | bytes 3145736 | tf_op jit(solution)/shard_map/ppermute | solution.py:14
  113.3 3.0 %collective-permute-done.2 = bf16[256,1024]{1,0:T(8,128)(2,1)} collective-permute-done((bf16[256,1024]{1,0:T(8,128)(2,1)}, bf16[256,1024]{1,0:T(8,128)(2,1)}, u32[]{:S(2)}, u32[]{:S(2)}) %collective-permute-start.2) | collective-permute-done | bytes 524320 | tf_op jit(solution)/shard_map/ppermute | solution.py:14
  116.3 3.8 %collective-permute-start.3 = (bf16[256,1024]{1,0:T(8,128)(2,1)}, bf16[256,1024]{1,0:T(8,128)(2,1)S(1)}, u32[]{:S(2)}, u32[]{:S(2)}) collective-permute-start(bf16[256,1024]{1,0:T(8,128)(2,1)} %collective-permute-done.2), channel_id=1, source_target_pairs={{0,28},{4,0},{8,4},{12,8},{16,12},{20,16},{24,20},{28,24},{1,29},{... | collective-permute-start | bytes 1572872 | tf_op jit(solution)/shard_map/ppermute | solution.py:14
  122.7 16.0 %collective-permute-done.6 = f32[256,1024]{1,0:T(8,128)} collective-permute-done((f32[256,1024]{1,0:T(8,128)}, f32[256,1024]{1,0:T(8,128)}, u32[]{:S(2)}, u32[]{:S(2)}) %collective-permute-start.6) | collective-permute-done | bytes 1048608 | tf_op jit(solution)/shard_map/ppermute | solution.py:14
  140.1 4.1 %collective-permute-start.7 = (f32[256,1024]{1,0:T(8,128)S(1)}, f32[256,1024]{1,0:T(8,128)S(1)}, u32[]{:S(2)}, u32[]{:S(2)}) collective-permute-start(f32[256,1024]{1,0:T(8,128)S(1)} %add.246), channel_id=1, source_target_pairs={{0,28},{4,0},{8,4},{12,8},{16,12},{20,16},{24,20},{28,24},{1,29},{... | collective-permute-start | bytes 3145736 | tf_op jit(solution)/shard_map/ppermute | solution.py:14
  146.9 3.0 %collective-permute-done.3 = bf16[256,1024]{1,0:T(8,128)(2,1)S(1)} collective-permute-done((bf16[256,1024]{1,0:T(8,128)(2,1)}, bf16[256,1024]{1,0:T(8,128)(2,1)S(1)}, u32[]{:S(2)}, u32[]{:S(2)}) %collective-permute-start.3) | collective-permute-done | bytes 524320 | tf_op jit(solution)/shard_map/ppermute | solution.py:14
  151.4 20.2 %collective-permute-done.7 = f32[256,1024]{1,0:T(8,128)S(1)} collective-permute-done((f32[256,1024]{1,0:T(8,128)S(1)}, f32[256,1024]{1,0:T(8,128)S(1)}, u32[]{:S(2)}, u32[]{:S(2)}) %collective-permute-start.7) | collective-permute-done | bytes 1048608 | tf_op jit(solution)/shard_map/ppermute | solution.py:14
  173.2 11.6 %fusion.63 = f32[3]{0:T(128)S(1)} fusion(f32[1]{0:T(128)} %bitcast.24, f32[1]{0:T(128)} %bitcast.23, f32[1]{0:T(128)} %bitcast.22, f32[1]{0:T(128)} %bitcast.27, f32[1]{0:T(128)} %bitcast.26, f32[1]{0:T(128)} %bitcast.25, f32[1]{0:T(128)} %bitcast.21, f32[1]{0:T(128)} %bitcast.20, f32[1]{0:T(128)} %bitcast.19, f32[1]{0:T(128)} %bitcast.18, f32[1]{0:T(128)} %bitcast.17, ...), kind=kLoop, calls=%fused_computation.151 | loop fusion | flops 51 | bytes 84 | tf_op jit(solution)/shard_map/add | solution.py:117
  186.5 32.2 %collective-permute-done.8 = f32[256,1024]{1,0:T(8,128)S(1)} collective-permute-done((f32[256,1024]{1,0:T(8,128)S(1)}, f32[256,1024]{1,0:T(8,128)S(1)}, u32[]{:S(2)}, u32[]{:S(2)}) %collective-permute-start.8) | collective-permute-done | bytes 1048608 | tf_op jit(solution)/shard_map/ppermute | solution.py:14
  220.5 6.8 %all-reduce.1 = (f32[1024]{0:T(1024)S(1)}, f32[3]{0:T(128)S(1)}) all-reduce(f32[1024]{0:T(1024)S(1)} %get-tuple-element.28, f32[3]{0:T(128)S(1)} %fusion.63), channel_id=1, replica_groups=mesh['dp'=8,'rep'=4] {'rep'}, use_global_device_ids=true, to_apply=%region_12.13 | all-reduce | flops 1027 | bytes 8216 | tf_op jit(solution)/shard_map/psum | solution.py:134
  227.3 21.0 %all-reduce = (f32[1024]{0:T(1024)}, f32[3]{0:T(128)S(1)}) all-reduce(f32[1024]{0:T(1024)S(1)} %get-tuple-element.25, f32[3]{0:T(128)S(1)} %get-tuple-element.26), channel_id=1, replica_groups=mesh['dp'=8,'rep'=4] {'dp'}, use_global_device_ids=true, to_apply=%region_13.14 | all-reduce | flops 1027 | bytes 8216 | tf_op jit(solution)/shard_map/psum | solution.py:134
  (77 shorter events, 30.0 us)
Async XLA Ops:
  1.6 22.7 %copy-start = (bf16[256,1024]{1,0:T(8,128)(2,1)S(1)}, bf16[256,1024]{1,0:T(8,128)(2,1)}, u32[]{:S(2)}) copy-start(bf16[256,1024]{1,0:T(8,128)(2,1)} %param.7) | copy-start | bytes 1572868
  19.4 4.9 %copy-start.2 = (f32[1024]{0:T(1024)S(1)}, f32[1024]{0:T(1024)}, u32[]{:S(2)}) copy-start(f32[1024]{0:T(1024)} %param.8) | copy-start | bytes 12292
  20.0 47.4 %all-to-all-start = ((s32[4,1,16]{2,1,0:T(1,128)}), s32[4,1,16]{2,1,0:T(1,128)S(1)}, u32[]{:S(2)}, u32[]{:S(2)}) async-start(s32[4,1,16]{2,1,0:T(1,128)} %bitcast.5), calls=%async_computation | async-start | bytes 4096 | tf_op jit(solution)/shard_map/all_to_all | solution.py:99
  24.5 5.3 %copy-start.1 = (bf16[256,1024]{1,0:T(8,128)(2,1)S(1)}, bf16[256,1024]{1,0:T(8,128)(2,1)}, u32[]{:S(2)}) copy-start(bf16[256,1024]{1,0:T(8,128)(2,1)} %param.6) | copy-start | bytes 1572868
  24.7 42.8 %collective-permute-start = (bf16[256,1024]{1,0:T(8,128)(2,1)S(1)}, bf16[256,1024]{1,0:T(8,128)(2,1)}, u32[]{:S(2)}, u32[]{:S(2)}) collective-permute-start(bf16[256,1024]{1,0:T(8,128)(2,1)S(1)} %fusion.77), channel_id=1, source_target_pairs={{0,28},{4,0},{8,4},{12,8},{16,12},{20,16},{24,20},{28,24},{1,29},{... | collective-permute-start | bytes 1572872 | tf_op jit(solution)/shard_map/ppermute | solution.py:14
  34.1 36.8 %collective-permute-start.4 = (f32[256,1024]{1,0:T(8,128)}, f32[256,1024]{1,0:T(8,128)}, u32[]{:S(2)}, u32[]{:S(2)}) collective-permute-start(f32[256,1024]{1,0:T(8,128)} %fusion.33), channel_id=1, source_target_pairs={{0,28},{4,0},{8,4},{12,8},{16,12},{20,16},{24,20},{28,24},{1,29},{... | collective-permute-start | bytes 3145736 | tf_op jit(solution)/shard_map/ppermute | solution.py:14
  50.4 0.5 copy-start.5
  67.5 15.1 %collective-permute-start.1 = (bf16[256,1024]{1,0:T(8,128)(2,1)}, bf16[256,1024]{1,0:T(8,128)(2,1)}, u32[]{:S(2)}, u32[]{:S(2)}) collective-permute-start(bf16[256,1024]{1,0:T(8,128)(2,1)} %collective-permute-done), channel_id=1, source_target_pairs={{0,28},{4,0},{8,4},{12,8},{16,12},{20,16},{24,20},{28,24},{1,29},{... | collective-permute-start | bytes 1572872 | tf_op jit(solution)/shard_map/ppermute | solution.py:14
  73.5 31.6 %collective-permute-start.5 = (f32[256,1024]{1,0:T(8,128)}, f32[256,1024]{1,0:T(8,128)}, u32[]{:S(2)}, u32[]{:S(2)}) collective-permute-start(f32[256,1024]{1,0:T(8,128)} %convolution_add_fusion), channel_id=1, source_target_pairs={{0,28},{4,0},{8,4},{12,8},{16,12},{20,16},{24,20},{28,24},{1,29},{... | collective-permute-start | bytes 3145736 | tf_op jit(solution)/shard_map/ppermute | solution.py:14
  76.4 34.8 %all-to-all-start.1 = ((bf16[4,16,1024]{2,1,0:T(8,128)(2,1)}), bf16[4,16,1024]{2,1,0:T(8,128)(2,1)S(1)}, u32[]{:S(2)}, u32[]{:S(2)}) async-start(bf16[4,16,1024]{2,1,0:T(8,128)(2,1)} %broadcast_select_fusion), calls=%async_computation.1 | async-start | bytes 262144 | tf_op jit(solution)/shard_map/all_to_all | solution.py:101
  85.2 31.1 %collective-permute-start.2 = (bf16[256,1024]{1,0:T(8,128)(2,1)}, bf16[256,1024]{1,0:T(8,128)(2,1)}, u32[]{:S(2)}, u32[]{:S(2)}) collective-permute-start(bf16[256,1024]{1,0:T(8,128)(2,1)} %collective-permute-done.1), channel_id=1, source_target_pairs={{0,28},{4,0},{8,4},{12,8},{16,12},{20,16},{24,20},{28,24},{1,29},{... | collective-permute-start | bytes 1572872 | tf_op jit(solution)/shard_map/ppermute | solution.py:14
  107.4 3.9 %copy-start.3 = (pred[64]{0:T(512)(128)(4,1)S(1)}, pred[64]{0:T(512)(128)(4,1)}, u32[]{:S(2)}) copy-start(pred[64]{0:T(512)(128)(4,1)} %broadcast_compare_fusion.2) | copy-start | bytes 196
  107.4 3.9 %copy-start.4 = (s32[64]{0:T(128)S(1)}, s32[64]{0:T(128)}, u32[]{:S(2)}) copy-start(s32[64]{0:T(128)} %scatter_custom_fusion) | copy-start | bytes 772
  107.4 31.4 %collective-permute-start.6 = (f32[256,1024]{1,0:T(8,128)}, f32[256,1024]{1,0:T(8,128)}, u32[]{:S(2)}, u32[]{:S(2)}) collective-permute-start(f32[256,1024]{1,0:T(8,128)} %add.245), channel_id=1, source_target_pairs={{0,28},{4,0},{8,4},{12,8},{16,12},{20,16},{24,20},{28,24},{1,29},{... | collective-permute-start | bytes 3145736 | tf_op jit(solution)/shard_map/ppermute | solution.py:14
  111.6 0.6 copy-start.6
  116.3 33.6 %collective-permute-start.3 = (bf16[256,1024]{1,0:T(8,128)(2,1)}, bf16[256,1024]{1,0:T(8,128)(2,1)S(1)}, u32[]{:S(2)}, u32[]{:S(2)}) collective-permute-start(bf16[256,1024]{1,0:T(8,128)(2,1)} %collective-permute-done.2), channel_id=1, source_target_pairs={{0,28},{4,0},{8,4},{12,8},{16,12},{20,16},{24,20},{28,24},{1,29},{... | collective-permute-start | bytes 1572872 | tf_op jit(solution)/shard_map/ppermute | solution.py:14
  140.1 31.5 %collective-permute-start.7 = (f32[256,1024]{1,0:T(8,128)S(1)}, f32[256,1024]{1,0:T(8,128)S(1)}, u32[]{:S(2)}, u32[]{:S(2)}) collective-permute-start(f32[256,1024]{1,0:T(8,128)S(1)} %add.246), channel_id=1, source_target_pairs={{0,28},{4,0},{8,4},{12,8},{16,12},{20,16},{24,20},{28,24},{1,29},{... | collective-permute-start | bytes 3145736 | tf_op jit(solution)/shard_map/ppermute | solution.py:14
  171.8 46.9 %collective-permute-start.8 = (f32[256,1024]{1,0:T(8,128)S(1)}, f32[256,1024]{1,0:T(8,128)S(1)}, u32[]{:S(2)}, u32[]{:S(2)}) collective-permute-start(f32[256,1024]{1,0:T(8,128)S(1)} %add.247), channel_id=1, source_target_pairs={{0,16},{4,20},{8,24},{12,28},{16,0},{20,4},{24,8},{28,12},{1,17},{... | collective-permute-start | bytes 3145736 | tf_op jit(solution)/shard_map/ppermute | solution.py:14
  248.3 0.5 copy-start.7
